TPU v7x, 256 devices: a whole 4x4x8 slice. The times are simulated.
256 devices in a mesh: row: 16 (over z, core), col: 16 (over x, y).
Axes of the slice: x: 4, y: 4, z: 8, core: 2. Of those that a mesh axis runs over, the one named last changes fastest.
Arguments:
- panel: float32 [16384, 128], P(('row', 'col')), as said below
- mobility: float32 [16384, 16384], P('row', 'col'), as said below
Outputs:
- updated: float32 [16384, 16384], P('row', 'col')
- panel_factor: float32 [128, 128], replicated
Inputs may be any that keep to these rules, and one draw needn't show every extreme that they name: Each row and each column of the panel has its own scale. `mobility`: Symmetric.
All inputs are finite; a program needn't handle non-finite values.
Results may differ from a plain program's by a relative error of at most 0.000076.
Values sent between devices are 32-bit elements; how exact they have to be, the bound alone decides.
No kernel may reach another device: no remote copies, remote signals or barrier semaphores. Data moves between devices by JAX's collectives and lax.ppermute only.
A program may use at most 64 MiB of HBM per device.

v0:
```python
import jax
import jax.numpy as jnp
from jax import lax
from jax.sharding import PartitionSpec as P


def spread(shard, axis, root):
    mine = lax.axis_index(axis) == root
    return lax.psum(jnp.where(mine, shard, jnp.zeros_like(shard)), axis)


def product(first_op, second_op):
    return jnp.dot(
        first_op, second_op, precision=lax.Precision.HIGHEST, preferred_element_type=jnp.float32
    )


def product_tn(first_op, second_op):
    return lax.dot_general(
        first_op,
        second_op,
        (((0,), (0,)), ((), ())),
        precision=lax.Precision.HIGHEST,
        preferred_element_type=jnp.float32,
    )


def product_nt(first_op, second_op):
    return lax.dot_general(
        first_op,
        second_op,
        (((1,), (1,)), ((), ())),
        precision=lax.Precision.HIGHEST,
        preferred_element_type=jnp.float32,
    )


def invert_core(core_matrix):
    identity = jnp.eye(core_matrix.shape[0], dtype=jnp.float32)

    def newton_step(index, approx):
        return product(approx, 2.0 * identity - product(core_matrix, approx))

    return lax.fori_loop(0, 12, newton_step, identity)


def correction_columns(block_rows_arr, block_ratio):
    root_index = lax.axis_index("col") * block_ratio + 0
    copies = spread(block_rows_arr, "row", root_index)
    return copies


def on_device(panel, mobility):
    piece_rows = panel.shape[0]
    width_cols = panel.shape[1]
    count_col = lax.axis_size("col")
    count_row = lax.axis_size("row")
    block_ratio = count_row // count_col
    row_index = lax.axis_index("row")
    col_index = lax.axis_index("col")
    block_rows = mobility.shape[0]
    block_cols = mobility.shape[1]
    first_row = (row_index * count_col + col_index) * piece_rows
    positions = first_row + jnp.arange(piece_rows, dtype=jnp.int32)
    selector = (jnp.arange(width_cols, dtype=jnp.int32)[:, None] == positions[None, :]).astype(
        jnp.float32
    )
    gram_term = product_tn(panel, panel)
    top_term = product(selector, panel)
    gram_sum, top_rows = lax.psum((gram_term, top_term), ("row", "col"))
    lower_factor = jnp.linalg.cholesky(gram_sum)
    panel_factor = lower_factor.T
    ortho_piece = jax.scipy.linalg.solve_triangular(lower_factor, panel.T, lower=True).T
    basis_piece = ortho_piece + selector.T
    top_ortho = jax.scipy.linalg.solve_triangular(lower_factor, top_rows.T, lower=True)
    core_matrix = jnp.eye(width_cols, dtype=jnp.float32) + top_ortho
    kernel = invert_core(core_matrix)
    everything = lax.all_gather(basis_piece, ("row", "col"), axis=0, tiled=True)
    basis_rows = lax.dynamic_slice_in_dim(everything, row_index * block_rows, block_rows, 0)
    basis_cols = lax.dynamic_slice_in_dim(everything, col_index * block_cols, block_cols, 0)
    partial_rows = product(mobility, basis_cols)
    spread_rows = product(lax.psum(partial_rows, "col"), kernel)
    inner_sum = lax.psum(product_tn(basis_rows, spread_rows), "row")
    inner = product_tn(kernel, inner_sum)
    correction_rows = spread_rows - 0.5 * product(basis_rows, inner)
    correction_cols = correction_columns(correction_rows, block_ratio)
    left_side = jnp.concatenate([basis_rows, correction_rows], axis=1)
    right_side = jnp.concatenate([correction_cols, basis_cols], axis=1)
    updated = mobility - product_nt(left_side, right_side)
    return (updated, panel_factor)


def solution(mesh):
    in_specs = (P(("row", "col"), None), P("row", "col"))
    out_specs = (P("row", "col"), P())
    return jax.shard_map(
        on_device, mesh=mesh, in_specs=in_specs, out_specs=out_specs, check_vma=False
    )
```

profile of v0, /device:TPU:1, one launch (start us, length us, event | category | flops | bytes accessed | tf_op | source)
XLA Modules:
  0.0 727.7 jit_solution(3753922273948830282)
XLA Ops:
  7.2 0.0 copy-start
  7.2 0.0 all-reduce.12.cloned.1.call-start
  7.2 0.7 copy-done
  7.9 0.9 fusion.18
  8.8 0.8 fusion.14
  9.6 0.0 all-reduce.12.cloned.1.call-update
  9.7 0.0 all-gather.2.cloned.1.call-start
  9.7 249.4 %all-reduce.12.cloned.1.call-done = (f32[128,128]{0,1:T(8,128)}, f32[128,128]{1,0:T(8,128)}) async-done(((f32[128,128]{0,1:T(8,128)}, f32[128,128]{1,0:T(8,128)}), (f32[128,128]{0,1:T(8,128)}, f32[128,128]{1,0:T(8,128)})) %all-reduce.12.cloned.1.call-update) | async-done | bytes 131088 | tf_op jit(solution)/shard_map/psum | solution.py:70
  259.1 0.9 copy.5
  260.0 0.9 fusion.12
  260.9 11.7 %cholesky.19 = f32[128,128]{1,0:T(8,128)S(1)} custom-call(f32[128,128]{1,0:T(8,128)S(1)} %fusion.12), custom_call_target="Cholesky" | custom-call | tf_op jit(solution)/shard_map/jit(cholesky)/cholesky | solution.py:71
  272.6 0.6 compare_reduce_fusion
  273.3 0.7 fusion.15
  273.9 9.8 %custom-call.10 = f32[1,128,128]{1,2,0:T(8,128)S(1)} custom-call(f32[1,128,128]{2,1,0:T(8,128)S(1)} %get-tuple-element.49), custom_call_target="InvertDiagBlocksLowerTriangular" | custom-call | tf_op jit(solution)/shard_map/jit(_solve_triangular)/triangular_solve | solution.py:73
  283.8 0.8 fusion.3
  284.6 0.0 all-gather.2.cloned.1.call-update
  284.6 0.0 all-reduce.6.cloned.1.call-start
  284.7 0.1 copy.6
  284.7 1.1 convolution_add_fusion
  285.9 115.3 %all-gather.2.cloned.1.call-done = f32[16384,128]{1,0:T(8,128)} async-done(((f32[64,128]{1,0:T(8,128)}), f32[16384,128]{1,0:T(8,128)}) %all-gather.2.cloned.1.call-update) | async-done | bytes 8388624 | tf_op jit(solution)/shard_map/all_gather | solution.py:78
  401.2 1.3 constant_dynamic-slice_fusion.1
  402.5 7.5 %convolution_bitcast_fusion.1 = f32[1024,128]{0,1:T(8,128)} fusion(f32[1024,128]{1,0:T(8,128)S(1)} %get-tuple-element.47, f32[1024,1024]{1,0:T(8,128)} %param.5), kind=kOutput, calls=%fused_computation.7 | convolution fusion | flops 1610612736 | bytes 5242880 | tf_op jit(solution)/shard_map/dot_general | solution.py:13
  409.9 0.0 all-reduce.6.cloned.1.call-update
  410.0 0.2 all-reduce.8.cloned.1.call-start
  410.2 7.1 while.11
  410.2 0.3 convolution_subtract_fusion.3
  410.5 0.3 convolution_bitcast_fusion.4
  410.8 0.3 convolution_subtract_fusion.3
  411.1 0.3 convolution_bitcast_fusion.4
  411.4 0.3 convolution_subtract_fusion.3
  411.7 0.3 convolution_bitcast_fusion.4
  412.0 0.3 convolution_subtract_fusion.3
  412.3 0.3 convolution_bitcast_fusion.4
  412.6 0.3 convolution_subtract_fusion.3
  412.9 0.3 convolution_bitcast_fusion.4
  413.2 0.3 convolution_subtract_fusion.3
  413.5 0.3 convolution_bitcast_fusion.4
  413.8 0.3 convolution_subtract_fusion.3
  414.0 0.3 convolution_bitcast_fusion.4
  414.4 0.3 convolution_subtract_fusion.3
  414.6 0.3 convolution_bitcast_fusion.4
  415.0 0.3 convolution_subtract_fusion.3
  415.2 0.3 convolution_bitcast_fusion.4
  415.6 0.3 convolution_subtract_fusion.3
  415.8 0.3 convolution_bitcast_fusion.4
  416.1 0.3 convolution_subtract_fusion.3
  416.4 0.3 convolution_bitcast_fusion.4
  416.7 0.3 convolution_subtract_fusion.3
  417.0 0.3 convolution_bitcast_fusion.4
  417.3 83.1 %all-reduce.6.cloned.1.call-done = f32[1024,128]{0,1:T(8,128)} async-done(((f32[1024,128]{0,1:T(8,128)}), f32[1024,128]{0,1:T(8,128)}) %all-reduce.6.cloned.1.call-update) | async-done | bytes 524304 | tf_op jit(solution)/shard_map/psum | solution.py:82
  500.4 1.6 fusion.19
  502.1 1.6 fusion.20
  503.7 0.0 all-reduce.8.cloned.1.call-update
  503.7 0.0 all-reduce.10.cloned.1.call-start
  503.8 0.2 copy.8
  504.0 99.9 %all-reduce.8.cloned.1.call-done = f32[128,128]{1,0:T(8,128)} async-done(((f32[128,128]{1,0:T(8,128)}), f32[128,128]{1,0:T(8,128)}) %all-reduce.8.cloned.1.call-update) | async-done | bytes 65552 | tf_op jit(solution)/shard_map/psum | solution.py:83
  603.9 1.0 fusion.21
  604.9 1.4 broadcast_select_fusion
  606.3 0.0 all-reduce.10.cloned.1.call-update
  606.3 0.7 copy.9
  607.1 107.4 %all-reduce.10.cloned.1.call-done = f32[1024,128]{1,0:T(8,128)} async-done(((f32[1024,128]{1,0:T(8,128)}), f32[1024,128]{1,0:T(8,128)}) %all-reduce.10.cloned.1.call-update) | async-done | bytes 524304 | tf_op jit(solution)/shard_map/psum | solution.py:9
  714.4 6.7 convolution_subtract_fusion.1
  (15 shorter events, 0.1 us)
Async XLA Ops:
  7.2 0.8 copy-start
  7.2 251.9 %all-reduce.12.cloned.1.call-start = ((), (), s32[]{:S(2)}) async-start(), calls=%async_computation.4 | async-start | bytes 262144 | tf_op jit(solution)/shard_map/psum | solution.py:70
  9.7 391.5 %all-gather.2.cloned.1.call-start = ((), (), s32[]{:S(2)}) async-start(), calls=%async_computation | async-start | bytes 8421376 | tf_op jit(solution)/shard_map/all_gather | solution.py:78
  284.6 215.8 %all-reduce.6.cloned.1.call-start = ((), (), s32[]{:S(2)}) async-start(), calls=%async_computation.1 | async-start | bytes 1048576 | tf_op jit(solution)/shard_map/psum | solution.py:82
  410.0 193.9 %all-reduce.8.cloned.1.call-start = ((), (), s32[]{:S(2)}) async-start(), calls=%async_computation.2 | async-start | bytes 131072 | tf_op jit(solution)/shard_map/psum | solution.py:83
  503.7 210.7 %all-reduce.10.cloned.1.call-start = ((), (), s32[]{:S(2)}) async-start(), calls=%async_computation.3 | async-start | bytes 1048576 | tf_op jit(solution)/shard_map/psum | solution.py:9
Sparse Core Ops, SparseCore 0:
  14.2 244.8 all-reduce.11
  284.7 116.4 all-gather.1
  410.1 90.2 all-reduce.5
  503.8 99.9 all-reduce.7
  606.6 107.7 all-reduce.9
where the time goes:
time: 728 us
  waiting for transfers between devices  655 us (90%)
  matrix products  30.2 us (4%)
  other arithmetic  23.7 us (3%)
  between operations  13.9 us (2%)
    psum x1, waiting for transfers between devices, on_device(): gram_sum, top_rows = lax.psum((gram_term, top_term), ('row', 'col'))  249 us
    all_gather x1, waiting for transfers between devices, on_device(): everything = lax.all_gather(basis_piece, ('row', 'col'), axis=0, tiled=True)  115 us
    psum x1, waiting for transfers between devices, spread(): return lax.psum(jnp.where(mine, shard, jnp.zeros_like(shard)), axis)  107 us
    psum x1, waiting for transfers between devices, on_device(): inner_sum = lax.psum(product_tn(basis_rows, spread_rows), 'row')  99.9 us
    psum x1, waiting for transfers between devices, on_device(): spread_rows = product(lax.psum(partial_rows, 'col'), kernel)  83.1 us
    dot_general x28, matrix products, product(): jnp.dot(first_op, second_op, precision=lax.Precision.HIGHEST, preferred_e...  17.9 us
  transfers between devices with their start and end apart: 5, of which 5 were waited for; matrix products, arithmetic and copies ran while one was open for 1% of the time, Pallas kernels for 0%

commit v1 on v0

--- a/solution.py
+++ b/solution.py
@@ -67,7 +67,7 @@
     )
     gram_term = product_tn(panel, panel)
     top_term = product(selector, panel)
-    gram_sum, top_rows = lax.psum((gram_term, top_term), ("row", "col"))
+    gram_sum, top_rows = lax.psum(lax.psum((gram_term, top_term), "row"), "col")
     lower_factor = jnp.linalg.cholesky(gram_sum)
     panel_factor = lower_factor.T
     ortho_piece = jax.scipy.linalg.solve_triangular(lower_factor, panel.T, lower=True).T

time: 728 us -> 697 us (0.957)
  waiting for transfers between devices: 655 us -> 623 us
    psum x1 -> x2, waiting for transfers between devices: 249 us -> 206 us  [on_device(): gram_sum, top_rows = lax.psum(lax.psum((gram_term, top_term), 'row'), 'col')]
  transfers between devices with their start and end apart: 5 -> 6, of which waited for: 5 -> 6; matrix products, arithmetic and copies ran while one was open for 1% -> 0% of each run, Pallas kernels for 0% -> 0%
where the time goes in v1:
time: 697 us; the launch traced here: 696 us
  waiting for transfers between devices  623 us (89%)
  matrix products  30.2 us (4%)
  other arithmetic  23.7 us (3%)
  between operations  14.2 us (2%)
    psum x2, waiting for transfers between devices, on_device(): gram_sum, top_rows = lax.psum(lax.psum((gram_term, top_term), 'row'), 'col')  206 us
    all_gather x1, waiting for transfers between devices, on_device(): everything = lax.all_gather(basis_piece, ('row', 'col'), axis=0, tiled=True)  120 us
    psum x1, waiting for transfers between devices, spread(): return lax.psum(jnp.where(mine, shard, jnp.zeros_like(shard)), axis)  107 us
    psum x1, waiting for transfers between devices, on_device(): inner_sum = lax.psum(product_tn(basis_rows, spread_rows), 'row')  99.9 us
    psum x1, waiting for transfers between devices, on_device(): spread_rows = product(lax.psum(partial_rows, 'col'), kernel)  90.2 us
    dot_general x28, matrix products, product(): jnp.dot(first_op, second_op, precision=lax.Precision.HIGHEST, preferred_e...  17.9 us
  transfers between devices with their start and end apart: 6, of which 6 were waited for; matrix products, arithmetic and copies ran while one was open for 0% of the time, Pallas kernels for 0%

profile of v1, /device:TPU:1, one launch (start us, length us, event | category | flops | bytes accessed | tf_op | source)
XLA Modules:
  0.0 696.4 jit_solution(14759294998624913125)
XLA Ops:
  7.2 0.0 all-reduce.16.cloned.1.call-start
  7.2 0.7 copy-done
  7.9 0.9 fusion.18
  8.8 0.8 fusion.14
  9.6 0.0 all-reduce.16.cloned.1.call-update
  9.7 0.0 all-reduce.8.cloned.1.call-start
  9.7 112.7 %all-reduce.16.cloned.1.call-done = (f32[128,128]{0,1:T(8,128)}, f32[128,128]{1,0:T(8,128)}) async-done(((f32[128,128]{0,1:T(8,128)}, f32[128,128]{1,0:T(8,128)}), (f32[128,128]{0,1:T(8,128)}, f32[128,128]{1,0:T(8,128)})) %all-reduce.16.cloned.1.call-update) | async-done | bytes 131088 | tf_op jit(solution)/shard_map/psum | solution.py:70
  122.4 0.0 all-reduce.8.cloned.1.call-update
  122.5 0.0 all-gather.2.cloned.1.call-start
  122.5 93.2 %all-reduce.8.cloned.1.call-done = f32[128,128]{0,1:T(8,128)} async-done(((f32[128,128]{0,1:T(8,128)}), f32[128,128]{0,1:T(8,128)}) %all-reduce.8.cloned.1.call-update) | async-done | bytes 65552 | tf_op jit(solution)/shard_map/psum | solution.py:70
  215.8 0.9 copy.5
  216.7 0.9 fusion.12
  217.5 11.7 %cholesky.19 = f32[128,128]{1,0:T(8,128)S(1)} custom-call(f32[128,128]{1,0:T(8,128)S(1)} %fusion.12), custom_call_target="Cholesky" | custom-call | tf_op jit(solution)/shard_map/jit(cholesky)/cholesky | solution.py:71
  229.3 0.6 compare_reduce_fusion
  229.9 0.7 fusion.15
  230.6 9.8 %custom-call.10 = f32[1,128,128]{1,2,0:T(8,128)S(1)} custom-call(f32[1,128,128]{2,1,0:T(8,128)S(1)} %get-tuple-element.51), custom_call_target="InvertDiagBlocksLowerTriangular" | custom-call | tf_op jit(solution)/shard_map/jit(_solve_triangular)/triangular_solve | solution.py:73
  240.4 0.8 fusion.3
  241.2 0.0 all-gather.2.cloned.1.call-update
  241.2 0.0 all-reduce.14.cloned.1.call-start
  241.3 119.8 %all-gather.2.cloned.1.call-done = f32[16384,128]{1,0:T(8,128)} async-done(((f32[64,128]{1,0:T(8,128)}), f32[16384,128]{1,0:T(8,128)}) %all-gather.2.cloned.1.call-update) | async-done | bytes 8388624 | tf_op jit(solution)/shard_map/all_gather | solution.py:78
  361.1 1.3 constant_dynamic-slice_fusion.1
  362.4 7.5 %convolution_bitcast_fusion.1 = f32[1024,128]{0,1:T(8,128)} fusion(f32[1024,128]{1,0:T(8,128)S(1)} %get-tuple-element.49, f32[1024,1024]{1,0:T(8,128)} %param.5), kind=kOutput, calls=%fused_computation.7 | convolution fusion | flops 1610612736 | bytes 5242880 | tf_op jit(solution)/shard_map/dot_general | solution.py:13
  369.8 0.0 all-reduce.14.cloned.1.call-update
  369.9 0.2 all-reduce.10.cloned.1.call-start
  370.1 0.1 copy.6
  370.2 90.2 %all-reduce.14.cloned.1.call-done = (f32[1024,128]{0,1:T(8,128)}, f32[128,128]{1,0:T(8,128)}) async-done(((f32[1024,128]{0,1:T(8,128)}, f32[128,128]{1,0:T(8,128)}), (f32[1024,128]{0,1:T(8,128)}, f32[128,128]{1,0:T(8,128)})) %all-reduce.14.cloned.1.call-update) | async-done | bytes 589840 | tf_op jit(solution)/shard_map/psum | solution.py:82
  460.4 1.1 convolution_add_fusion
  461.5 7.1 %while.11 = (s32[]{:T(128)}, f32[128,128]{0,1:T(8,128)S(1)}, f32[128,128]{1,0:T(8,128)S(1)}, s32[]{:T(128)}) while((s32[]{:T(128)}, f32[128,128]{0,1:T(8,128)S(1)}, f32[128,128]{1,0:T(8,128)S(1)}, s32[]{:T(128)}) %tuple.30), condition=%wide.region_8.9_spmd.clone, body=%wide.region_7.8_spmd.clone.sunk | while | flops 50380800 | bytes 524341 | solution.py:44
  461.5 0.3 convolution_subtract_fusion.3
  461.8 0.3 convolution_bitcast_fusion.4
  462.1 0.3 convolution_subtract_fusion.3
  462.4 0.3 convolution_bitcast_fusion.4
  462.7 0.3 convolution_subtract_fusion.3
  463.0 0.3 convolution_bitcast_fusion.4
  463.3 0.3 convolution_subtract_fusion.3
  463.6 0.3 convolution_bitcast_fusion.4
  463.9 0.3 convolution_subtract_fusion.3
  464.2 0.3 convolution_bitcast_fusion.4
  464.5 0.3 convolution_subtract_fusion.3
  464.8 0.3 convolution_bitcast_fusion.4
  465.1 0.3 convolution_subtract_fusion.3
  465.4 0.3 convolution_bitcast_fusion.4
  465.7 0.3 convolution_subtract_fusion.3
  466.0 0.3 convolution_bitcast_fusion.4
  466.3 0.3 convolution_subtract_fusion.3
  466.5 0.3 convolution_bitcast_fusion.4
  466.9 0.3 convolution_subtract_fusion.3
  467.1 0.3 convolution_bitcast_fusion.4
  467.5 0.3 convolution_subtract_fusion.3
  467.7 0.3 convolution_bitcast_fusion.4
  468.1 0.3 convolution_subtract_fusion.3
  468.3 0.3 convolution_bitcast_fusion.4
  468.6 1.6 fusion.19
  470.3 1.6 fusion.20
  471.9 0.0 all-reduce.10.cloned.1.call-update
  471.9 0.0 all-reduce.12.cloned.1.call-start
  472.0 0.2 copy.8
  472.2 99.9 %all-reduce.10.cloned.1.call-done = f32[128,128]{1,0:T(8,128)} async-done(((f32[128,128]{1,0:T(8,128)}), f32[128,128]{1,0:T(8,128)}) %all-reduce.10.cloned.1.call-update) | async-done | bytes 65552 | tf_op jit(solution)/shard_map/psum | solution.py:83
  572.1 1.0 fusion.21
  573.2 1.4 broadcast_select_fusion
  574.5 0.0 all-reduce.12.cloned.1.call-update
  574.5 0.7 copy.9
  575.3 107.5 %all-reduce.12.cloned.1.call-done = f32[1024,128]{1,0:T(8,128)} async-done(((f32[1024,128]{1,0:T(8,128)}), f32[1024,128]{1,0:T(8,128)}) %all-reduce.12.cloned.1.call-update) | async-done | bytes 524304 | tf_op jit(solution)/shard_map/psum | solution.py:9
  682.8 6.7 convolution_subtract_fusion.1
  (16 shorter events, 0.1 us)
Async XLA Ops:
  7.2 0.8 copy-start
  7.2 115.3 %all-reduce.16.cloned.1.call-start = ((), (), s32[]{:S(2)}) async-start(), calls=%async_computation.5 | async-start | bytes 262144 | tf_op jit(solution)/shard_map/psum | solution.py:70
  9.7 206.1 %all-reduce.8.cloned.1.call-start = ((), (), s32[]{:S(2)}) async-start(), calls=%async_computation | async-start | bytes 131072 | tf_op jit(solution)/shard_map/psum | solution.py:70
  122.5 238.6 %all-gather.2.cloned.1.call-start = ((), (), s32[]{:S(2)}) async-start(), calls=%async_computation.1 | async-start | bytes 8421376 | tf_op jit(solution)/shard_map/all_gather | solution.py:78
  241.2 219.1 %all-reduce.14.cloned.1.call-start = ((), (), s32[]{:S(2)}) async-start(), calls=%async_computation.4 | async-start | bytes 1179648 | tf_op jit(solution)/shard_map/psum | solution.py:82
  369.9 202.3 %all-reduce.10.cloned.1.call-start = ((), (), s32[]{:S(2)}) async-start(), calls=%async_computation.2 | async-start | bytes 131072 | tf_op jit(solution)/shard_map/psum | solution.py:83
  471.9 210.8 %all-reduce.12.cloned.1.call-start = ((), (), s32[]{:S(2)}) async-start(), calls=%async_computation.3 | async-start | bytes 1048576 | tf_op jit(solution)/shard_map/psum | solution.py:9
Sparse Core Ops, SparseCore 0:
  10.9 111.4 all-reduce.15
  126.0 89.7 all-reduce.7
  241.4 119.6 all-gather.1
  370.0 90.3 all-reduce.13
  472.0 100.0 all-reduce.9
  575.0 107.7 all-reduce.11
